TPU v7x, 32 devices: a whole 2x2x4 slice. The times are simulated.
32 devices in a mesh: groups: 2 (over x), tensor: 2 (over core), query: 8 (over z, y).
Axes of the slice: x: 2, y: 2, z: 4, core: 2. Of those that a mesh axis runs over, the one named last changes fastest.
Arguments:
- query_tokens: bfloat16 [1024, 1024], P(('groups', 'tensor', 'query')), parts along dimension 0, may hold values from -6 to 6
- ln_gain: float32 [1024], replicated, may hold values from 0.1 to 1.9
- inner_weight: bfloat16 [1024, 65536], P(None, ('tensor', 'query')), may hold values from -0.1875 to 0.1875
- outer_weight: bfloat16 [65536, 1024], P(('tensor', 'query')), may hold values from -0.03125 to 0.03125
- final_gain: float32 [1024], replicated, may hold values from 0.1 to 1.9
- projection: bfloat16 [1024, 128], replicated, may hold values from -0.1875 to 0.1875
- segment_ids: int32 [1024], P('groups'), parts along dimension 0, may hold values from 0 to 31, never falling along the last dimension, each value on 1 to 32 neighbouring positions
- index_vectors: bfloat16 [131072, 128], P(('groups', 'tensor', 'query')), parts along dimension 0, may hold values from -6 to 6
- doc_ids: int32 [131072], P(('groups', 'tensor', 'query')), parts along dimension 0, may hold values from 0 to 127, as said below
Outputs:
- scores: float32 [32, 4096], P(None, ('groups', 'tensor', 'query')), parts along dimension 1
There are 2 independent parts, one for each index of `groups`. A program takes and returns all parts, laid end to end along the dimension named above; an argument that names none is the same for every part. Nothing has to cross between parts.
Inputs may be any that keep to these rules, and one draw needn't show every extreme that they name: `doc_ids`: within each shard of 4096 tokens the slot numbers never fall, start at 0 and leave no slot out up to the shard's largest; some shard uses all 128 slots. `segment_ids`: every query number appears; a query's tokens stand together.
All inputs are finite; a program needn't handle non-finite values.
Results may differ from a plain program's by a relative error of at most 0.0011.
Values may be sent and summed in bfloat16 or wider, within the bound.
No kernel may reach another device: no remote copies, remote signals or barrier semaphores. Data moves between devices by JAX's collectives and lax.ppermute only.
A program may use at most 128 MiB of HBM per device.

v0:
```python
import jax
import jax.numpy as jnp
from jax import lax
from jax.sharding import PartitionSpec as P

DOC_DEV = 128
EPSILON = 1e-06


def rms_rows(values, gain):
    mean_square = jnp.mean(values * values, axis=-1, keepdims=True)
    return values * lax.rsqrt(mean_square + EPSILON) * gain


def project_rows(mixed, final_gain, projection):
    final = rms_rows(mixed, final_gain).astype(jnp.bfloat16)
    projected = jnp.dot(final, projection, preferred_element_type=jnp.float32)
    scaled = projected * lax.rsqrt(jnp.sum(projected * projected, axis=-1, keepdims=True) + EPSILON)
    return scaled.astype(jnp.bfloat16)


def score_block(totals, query_rows, segment_rows, index_vectors, doc_ids, present):
    sims = jnp.einsum("jp,tp->jt", index_vectors, query_rows, preferred_element_type=jnp.float32)
    best = jax.ops.segment_max(sims, doc_ids, num_segments=totals.shape[1])
    best = jnp.where(present[:, None], best, 0.0)
    member = (segment_rows[None, :] == lax.iota(jnp.int32, totals.shape[0])[:, None]).astype(
        jnp.float32
    )
    return totals + jnp.einsum("qt,dt->qd", member, best, precision=lax.Precision.HIGHEST)


def score_rows(totals, query_rows, segment_rows, index_vectors, doc_ids, present):
    count_rows = query_rows.shape[0]
    if count_rows > 512 and count_rows % 512 == 0:
        blocks = count_rows // 512

        def block_step(carry, inputs):
            return (score_block(carry, inputs[0], inputs[1], index_vectors, doc_ids, present), None)

        stacked = (
            query_rows.reshape(blocks, 512, query_rows.shape[1]),
            segment_rows.reshape(blocks, 512),
        )
        totals, unused = lax.scan(block_step, totals, stacked)
        return totals
    return score_block(totals, query_rows, segment_rows, index_vectors, doc_ids, present)


def on_device(
    query_tokens,
    ln_gain,
    inner_weight,
    outer_weight,
    final_gain,
    projection,
    segment_ids,
    index_vectors,
    doc_ids,
):
    queries = segment_ids.shape[0] // 16
    present = jnp.any(doc_ids[:, None] == lax.iota(jnp.int32, DOC_DEV)[None, :], axis=0)
    empty = jnp.zeros((queries, DOC_DEV), jnp.float32)
    gathered = lax.all_gather(query_tokens, ("tensor", "query"), axis=0, tiled=True)
    normed = rms_rows(gathered.astype(jnp.float32), ln_gain).astype(jnp.bfloat16)
    hidden = jnp.maximum(
        jnp.dot(normed, inner_weight, preferred_element_type=jnp.float32), 0.0
    ).astype(jnp.bfloat16)
    own_out = lax.psum_scatter(
        jnp.dot(hidden, outer_weight, preferred_element_type=jnp.float32),
        ("tensor", "query"),
        scatter_dimension=0,
        tiled=True,
    )
    own_vectors = project_rows(query_tokens.astype(jnp.float32) + own_out, final_gain, projection)
    totals = score_rows(
        empty,
        lax.all_gather(own_vectors, ("tensor", "query"), axis=0, tiled=True),
        segment_ids,
        index_vectors,
        doc_ids,
        present,
    )
    lengths = jnp.sum(
        (segment_ids[None, :] == lax.iota(jnp.int32, queries)[:, None]).astype(jnp.float32), axis=1
    )
    return totals / lengths[:, None]


def solution(mesh):
    return jax.shard_map(
        on_device,
        mesh=mesh,
        in_specs=(
            P(("groups", "tensor", "query"), None),
            P(),
            P(None, ("tensor", "query")),
            P(("tensor", "query"), None),
            P(),
            P(),
            P("groups"),
            P(("groups", "tensor", "query"), None),
            P(("groups", "tensor", "query")),
        ),
        out_specs=P(None, ("groups", "tensor", "query")),
        check_vma=False,
    )
```

profile of v0, /device:TPU:1, one launch (start us, length us, event | category | flops | bytes accessed | tf_op | source)
XLA Modules:
  0.0 204.2 jit_solution(15623690360071753148)
XLA Ops:
  6.5 0.0 copy-start
  6.5 0.0 all-gather.2.cloned.1.call-start
  6.5 0.7 all-gather.2.cloned.1.call-update
  7.3 0.0 reduce-scatter.2.cloned.1.call-start
  7.3 42.6 %all-gather.2.cloned.1.call-done = bf16[512,1024]{1,0:T(8,128)(2,1)} async-done(((bf16[32,1024]{1,0:T(8,128)(2,1)}), bf16[512,1024]{1,0:T(8,128)(2,1)}) %all-gather.2.cloned.1.call-update) | async-done | bytes 1048592 | tf_op jit(solution)/shard_map/all_gather | solution.py:63
  49.9 1.5 fusion.2
  51.4 0.0 copy-start.4
  51.4 0.0 copy-start.3
  51.4 0.0 copy-start.1
  51.5 0.0 copy-start.2
  51.5 0.0 copy-start.5
  51.5 16.4 %fusion.18 = f32[512,1024]{1,0:T(8,128)} fusion(bf16[4096,1024]{1,0:T(8,128)(2,1)} %param.12, bf16[1024,4096]{1,0:T(8,128)(2,1)} %param.11, bf16[512,1024]{1,0:T(8,128)(2,1)} %all-gather.2.cloned.1.call-done, f32[1024]{0:T(1024)} %param.10, f32[512]{0:T(512)S(1)} %add_rsqrt_fusion), kind=kOutput, calls=%fused_computation.33 | convolution fusion | flops 8596226048 | bytes 19929088 | tf_op jit(solution)/shard_map/dot_general | solution.py:69
  67.9 0.0 reduce-scatter.2.cloned.1.call-update
  67.9 0.0 copy-done.4
  67.9 0.1 convert_reduce_fusion
  68.0 0.0 copy-done.3
  68.0 1.9 fusion.5
  69.9 56.7 %reduce-scatter.2.cloned.1.call-done = f32[32,1024]{1,0:T(8,128)} async-done(((f32[512,1024]{1,0:T(8,128)}), f32[32,1024]{1,0:T(8,128)}) %reduce-scatter.2.cloned.1.call-update) | async-done | bytes 131088 | tf_op jit(solution)/shard_map/reduce_scatter | solution.py:68
  126.6 0.0 copy-done.1
  126.6 1.0 multiply_reduce_fusion
  127.6 0.0 copy-done.2
  127.7 0.0 copy-done.5
  127.7 1.2 multiply_reduce_fusion.1
  128.9 0.1 multiply_convert_fusion.2
  129.0 33.3 %all_gather.7 = bf16[512,128]{1,0:T(8,128)(2,1)S(1)} all-gather(bf16[32,128]{1,0:T(8,128)(2,1)S(1)} %multiply_convert_fusion.2), channel_id=1, replica_groups=mesh['groups'=2,'tensor'=2,'query'=8] {'tensor','query'}, dimensions={0}, use_global_device_ids=true | all-gather | bytes 139264 | tf_op jit(solution)/shard_map/all_gather | solution.py:77
  162.3 0.0 copy-done
  162.3 4.5 %fusion.19 = f32[512,4096]{0,1:T(8,128)} fusion(bf16[512,128]{1,0:T(8,128)(2,1)S(1)} %all_gather.7, bf16[4096,128]{1,0:T(8,128)(2,1)S(1)} %copy-done), kind=kOutput, calls=%fused_computation.34 | convolution fusion | flops 536870912 | bytes 9568256 | tf_op jit(solution)/shard_map/jp,tp->jt/dot_general | solution.py:23
  166.8 29.6 %scatter_custom_fusion = f32[128,512]{1,0:T(8,128)S(1)} fusion(s32[4096]{0:T(1024)S(1)} %copy-done.3, f32[512,4096]{0,1:T(8,128)} %fusion.19, f32[]{:T(128)} %constant.6.clone.1), kind=kCustom, calls=%fused_computation.1 | custom fusion | flops 2097152 | bytes 8650756 | tf_op jit(solution)/shard_map/scatter-max | solution.py:24
  196.4 0.9 convolution_divide_fusion
  (3 shorter events, 0.0 us)
Async XLA Ops:
  6.5 155.8 %copy-start = (bf16[4096,128]{1,0:T(8,128)(2,1)S(1)}, bf16[4096,128]{1,0:T(8,128)(2,1)}, u32[]{:S(2)}) copy-start(bf16[4096,128]{1,0:T(8,128)(2,1)} %param.16) | copy-start | bytes 3145732
  6.5 43.4 %all-gather.2.cloned.1.call-start = ((), (), s32[]{:S(2)}) async-start(), calls=%async_computation.1 | async-start | bytes 1114112 | tf_op jit(solution)/shard_map/all_gather | solution.py:63
  7.3 119.3 %reduce-scatter.2.cloned.1.call-start = ((), (), s32[]{:S(2)}) async-start(), calls=%async_computation.2 | async-start | bytes 2228224 | tf_op jit(solution)/shard_map/reduce_scatter | solution.py:68
  51.4 16.5 %copy-start.4 = (s32[512]{0:T(512)S(1)}, s32[512]{0:T(512)}, u32[]{:S(2)}) copy-start(s32[512]{0:T(512)} %param.15) | copy-start | bytes 6148
  51.4 16.6 %copy-start.3 = (s32[4096]{0:T(1024)S(1)}, s32[4096]{0:T(1024)}, u32[]{:S(2)}) copy-start(s32[4096]{0:T(1024)} %param.17) | copy-start | bytes 49156
  51.4 75.2 %copy-start.1 = (bf16[32,1024]{1,0:T(8,128)(2,1)S(1)}, bf16[32,1024]{1,0:T(8,128)(2,1)}, u32[]{:S(2)}) copy-start(bf16[32,1024]{1,0:T(8,128)(2,1)} %param.9) | copy-start | bytes 196612
  51.5 76.2 %copy-start.2 = (bf16[1024,128]{1,0:T(8,128)(2,1)S(1)}, bf16[1024,128]{1,0:T(8,128)(2,1)}, u32[]{:S(2)}) copy-start(bf16[1024,128]{1,0:T(8,128)(2,1)} %param.14) | copy-start | bytes 786436
  51.5 76.2 %copy-start.5 = (f32[1024]{0:T(1024)S(1)}, f32[1024]{0:T(1024)}, u32[]{:S(2)}) copy-start(f32[1024]{0:T(1024)} %param.13) | copy-start | bytes 12292
Sparse Core Ops, SparseCore 0:
  9.5 40.3 all-gather.1
  68.0 58.5 reduce-scatter.1
where the time goes:
time: 204 us
  waiting for transfers between devices  100 us (49%)
  other arithmetic  34.2 us (17%)
  blocking collectives  33.3 us (16%)
  matrix products  23.1 us (11%)
  between operations  13.5 us (7%)
    reduce_scatter x1, waiting for transfers between devices, on_device(): lax.psum_scatter(jnp.dot(hidden, outer_weight, preferred_element_type=jnp...  56.7 us
    all_gather x1, waiting for transfers between devices, on_device(): lax.all_gather(query_tokens, ('tensor', 'query'), axis=0, tiled=True)  42.6 us
    all_gather x1, blocking collectives, on_device(): lax.all_gather(own_vectors, ('tensor', 'query'), axis=0, tiled=True)  33.3 us
    another operation x1, other arithmetic, score_block(): best = jax.ops.segment_max(sims, doc_ids, num_segments=totals.shape[1])  29.6 us
    dot_general x1, matrix products, on_device(): jnp.dot(hidden, outer_weight, preferred_element_type=jnp.float32)  16.4 us
    dot_general x1, matrix products, score_block(): jnp.einsum('jp,tp->jt', index_vectors, query_rows, preferred_element_type...  4.47 us
  transfers between devices with their start and end apart: 2, of which 2 were waited for; matrix products, arithmetic and copies ran while one was open for 1% of the time, Pallas kernels for 0%

commit v1 on v0

--- a/solution.py
+++ b/solution.py
@@ -1,3 +1,4 @@
+import functools
 import jax
 import jax.numpy as jnp
 from jax import lax
@@ -5,6 +6,43 @@
 
 DOC_DEV = 128
 EPSILON = 1e-06
+
+
+def _do_lanes(sample, which_axis):
+    a_now, new, base_arr = (lax.axis_size(which_axis), lax.axis_index(which_axis), sample.shape[0])
+    made = []
+    for src_i, it in enumerate(sample.shape):
+        made.append(it * a_now if src_i == 0 else it)
+    block_next = before = sample
+    h = 1
+    o_now = lax.dynamic_update_slice_in_dim(
+        jnp.zeros(made, sample.dtype), sample, new * base_arr, axis=0
+    )
+    while h < a_now // 2 + 1:
+        slots = []
+        src_i = 0
+        while src_i < a_now:
+            slots.append((src_i, (src_i + 1) % a_now))
+            src_i += 1
+        block_next = lax.ppermute(block_next, which_axis, slots)
+        o_now = lax.dynamic_update_slice_in_dim(
+            o_now, block_next, (new - h) % a_now * base_arr, axis=0
+        )
+        if 2 * h < a_now:
+            block_list = []
+            src_i = 0
+            while src_i < a_now:
+                block_list.append((src_i, (src_i - 1) % a_now))
+                src_i = src_i + 1
+            before = lax.ppermute(before, which_axis, block_list)
+            o_now = lax.dynamic_update_slice_in_dim(
+                o_now, before, (new + h) % a_now * base_arr, axis=0
+            )
+        h = h + 1
+    return o_now
+
+
+page_supply_all = functools.partial(_do_lanes, which_axis=("tensor", "query"))
 
 
 def rms_rows(values, gain):
@@ -73,12 +111,7 @@
     )
     own_vectors = project_rows(query_tokens.astype(jnp.float32) + own_out, final_gain, projection)
     totals = score_rows(
-        empty,
-        lax.all_gather(own_vectors, ("tensor", "query"), axis=0, tiled=True),
-        segment_ids,
-        index_vectors,
-        doc_ids,
-        present,
+        empty, page_supply_all(own_vectors), segment_ids, index_vectors, doc_ids, present
     )
     lengths = jnp.sum(
         (segment_ids[None, :] == lax.iota(jnp.int32, queries)[:, None]).astype(jnp.float32), axis=1

time: 204 us -> 220 us (1.078); the launches traced: 204 us -> 217 us
  blocking collectives: 33.3 us -> 0 us
  starting transfers between devices: 0.04 us -> 31.2 us
  waiting for transfers between devices: 100 us -> 115 us
    all_gather x1 -> x0, blocking collectives: 33.3 us -> none  [on_device(): lax.all_gather(own_vectors, ('tensor', 'query'), axis=0, tiled=True)]
    ppermute x0 -> x15, starting transfers between devices: none -> 31.1 us  [the longest x7 30.3 us: _do_lanes(): before = lax.ppermute(before, which_axis, block_list)]
    ppermute x0 -> x15, waiting for transfers between devices: none -> 15 us  [the longest x8 14.9 us: _do_lanes(): block_next = lax.ppermute(block_next, which_axis, slots)]
  transfers between devices with their start and end apart: 2 -> 17, of which waited for: 2 -> 10; matrix products, arithmetic and copies ran while one was open for 1% -> 1% of each run, Pallas kernels for 0% -> 0%
where the time goes in v1:
time: 220 us; the launch traced here: 217 us
  waiting for transfers between devices  115 us (52%)
  other arithmetic  34.5 us (16%)
  starting transfers between devices  31.2 us (14%)
  matrix products  23.1 us (10%)
  between operations  13.6 us (6%)
    reduce_scatter x1, waiting for transfers between devices, on_device(): lax.psum_scatter(jnp.dot(hidden, outer_weight, preferred_element_type=jnp...  56.6 us
    all_gather x1, waiting for transfers between devices, on_device(): lax.all_gather(query_tokens, ('tensor', 'query'), axis=0, tiled=True)  42.6 us
    ppermute x7, starting transfers between devices, _do_lanes(): before = lax.ppermute(before, which_axis, block_list)  30.3 us
    another operation x1, other arithmetic, score_block(): best = jax.ops.segment_max(sims, doc_ids, num_segments=totals.shape[1])  29.9 us
    dot_general x1, matrix products, on_device(): jnp.dot(hidden, outer_weight, preferred_element_type=jnp.float32)  16.4 us
    ppermute x8, waiting for transfers between devices, _do_lanes(): block_next = lax.ppermute(block_next, which_axis, slots)  14.9 us
    dot_general x1, matrix products, score_block(): jnp.einsum('jp,tp->jt', index_vectors, query_rows, preferred_element_type...  4.49 us
  transfers between devices with their start and end apart: 17, of which 10 were waited for; matrix products, arithmetic and copies ran while one was open for 1% of the time, Pallas kernels for 0%

profile of v1, /device:TPU:1, one launch (start us, length us, event | category | flops | bytes accessed | tf_op | source)
XLA Modules:
  0.0 217.4 jit_solution(15969977587433808642)
XLA Ops:
  6.5 0.7 all-gather.2.cloned.1.call-update
  7.3 0.0 reduce-scatter.2.cloned.1.call-start
  7.3 42.6 %all-gather.2.cloned.1.call-done = bf16[512,1024]{1,0:T(8,128)(2,1)} async-done(((bf16[32,1024]{1,0:T(8,128)(2,1)}), bf16[512,1024]{1,0:T(8,128)(2,1)}) %all-gather.2.cloned.1.call-update) | async-done | bytes 1048592 | tf_op jit(solution)/shard_map/all_gather | solution.py:101
  49.9 1.5 fusion.2
  51.4 0.0 copy-start.4
  51.4 0.0 copy-start.3
  51.4 0.0 copy-start.1
  51.5 0.0 copy-start.2
  51.5 0.0 copy-start.5
  51.5 16.4 %fusion.18 = f32[512,1024]{1,0:T(8,128)} fusion(bf16[4096,1024]{1,0:T(8,128)(2,1)} %param.12, bf16[1024,4096]{1,0:T(8,128)(2,1)} %param.11, bf16[512,1024]{1,0:T(8,128)(2,1)} %all-gather.2.cloned.1.call-done, f32[1024]{0:T(1024)} %param.10, f32[512]{0:T(512)S(1)} %add_rsqrt_fusion), kind=kOutput, calls=%fused_computation.49 | convolution fusion | flops 8596226048 | bytes 19929088 | tf_op jit(solution)/shard_map/dot_general | solution.py:107
  67.9 0.0 reduce-scatter.2.cloned.1.call-update
  68.0 0.1 convert_reduce_fusion
  68.1 1.9 fusion.5
  70.0 56.6 %reduce-scatter.2.cloned.1.call-done = f32[32,1024]{1,0:T(8,128)} async-done(((f32[512,1024]{1,0:T(8,128)}), f32[32,1024]{1,0:T(8,128)}) %reduce-scatter.2.cloned.1.call-update) | async-done | bytes 131088 | tf_op jit(solution)/shard_map/reduce_scatter | solution.py:106
  126.6 1.0 multiply_reduce_fusion
  127.7 1.2 multiply_reduce_fusion.1
  128.9 0.1 constant_dynamic-update-slice_fusion.15
  129.0 0.8 collective-permute-start
  129.8 3.7 %collective-permute-start.1 = (bf16[32,128]{1,0:T(8,128)(2,1)S(1)}, bf16[32,128]{1,0:T(8,128)(2,1)S(1)}, u32[]{:S(2)}, u32[]{:S(2)}) collective-permute-start(bf16[32,128]{1,0:T(8,128)(2,1)S(1)} %get-tuple-element.6), channel_id=1, source_target_pairs={{0,15},{1,0},{2,1},{3,2},{4,3},{5,4},{6,5},{7,6},{8,7},{9,8},{10,9... | collective-permute-start | bytes 24584 | tf_op jit(solution)/shard_map/ppermute | solution.py:37
  133.5 1.3 collective-permute-done
  134.8 0.0 collective-permute-start.2
  134.8 0.0 collective-permute-done.1
  134.8 4.4 %collective-permute-start.3 = (bf16[32,128]{1,0:T(8,128)(2,1)S(1)}, bf16[32,128]{1,0:T(8,128)(2,1)S(1)}, u32[]{:S(2)}, u32[]{:S(2)}) collective-permute-start(bf16[32,128]{1,0:T(8,128)(2,1)S(1)} %collective-permute-done.1), channel_id=1, source_target_pairs={{0,15},{1,0},{2,1},{3,2},{4,3},{5,4},{6,5},{7,6},{8,7},{9,8},{10,9... | collective-permute-start | bytes 24584 | tf_op jit(solution)/shard_map/ppermute | solution.py:37
  139.3 1.3 collective-permute-done.2
  140.6 0.0 collective-permute-start.4
  140.6 0.0 collective-permute-done.3
  140.6 4.4 %collective-permute-start.5 = (bf16[32,128]{1,0:T(8,128)(2,1)S(1)}, bf16[32,128]{1,0:T(8,128)(2,1)S(1)}, u32[]{:S(2)}, u32[]{:S(2)}) collective-permute-start(bf16[32,128]{1,0:T(8,128)(2,1)S(1)} %collective-permute-done.3), channel_id=1, source_target_pairs={{0,15},{1,0},{2,1},{3,2},{4,3},{5,4},{6,5},{7,6},{8,7},{9,8},{10,9... | collective-permute-start | bytes 24584 | tf_op jit(solution)/shard_map/ppermute | solution.py:37
  145.0 1.3 collective-permute-done.4
  146.3 0.0 collective-permute-start.6
  146.4 0.0 collective-permute-done.5
  146.4 4.4 %collective-permute-start.7 = (bf16[32,128]{1,0:T(8,128)(2,1)S(1)}, bf16[32,128]{1,0:T(8,128)(2,1)S(1)}, u32[]{:S(2)}, u32[]{:S(2)}) collective-permute-start(bf16[32,128]{1,0:T(8,128)(2,1)S(1)} %collective-permute-done.5), channel_id=1, source_target_pairs={{0,15},{1,0},{2,1},{3,2},{4,3},{5,4},{6,5},{7,6},{8,7},{9,8},{10,9... | collective-permute-start | bytes 24584 | tf_op jit(solution)/shard_map/ppermute | solution.py:37
  150.8 1.3 collective-permute-done.6
  152.1 0.0 collective-permute-start.8
  152.1 0.0 collective-permute-done.7
  152.1 4.4 %collective-permute-start.9 = (bf16[32,128]{1,0:T(8,128)(2,1)S(1)}, bf16[32,128]{1,0:T(8,128)(2,1)S(1)}, u32[]{:S(2)}, u32[]{:S(2)}) collective-permute-start(bf16[32,128]{1,0:T(8,128)(2,1)S(1)} %collective-permute-done.7), channel_id=1, source_target_pairs={{0,15},{1,0},{2,1},{3,2},{4,3},{5,4},{6,5},{7,6},{8,7},{9,8},{10,9... | collective-permute-start | bytes 24584 | tf_op jit(solution)/shard_map/ppermute | solution.py:37
  156.6 1.3 collective-permute-done.8
  157.9 0.0 collective-permute-start.10
  157.9 0.0 collective-permute-done.9
  157.9 4.4 %collective-permute-start.11 = (bf16[32,128]{1,0:T(8,128)(2,1)S(1)}, bf16[32,128]{1,0:T(8,128)(2,1)S(1)}, u32[]{:S(2)}, u32[]{:S(2)}) collective-permute-start(bf16[32,128]{1,0:T(8,128)(2,1)S(1)} %collective-permute-done.9), channel_id=1, source_target_pairs={{0,15},{1,0},{2,1},{3,2},{4,3},{5,4},{6,5},{7,6},{8,7},{9,8},{10,9... | collective-permute-start | bytes 24584 | tf_op jit(solution)/shard_map/ppermute | solution.py:37
  162.4 1.3 collective-permute-done.10
  163.7 0.0 collective-permute-done.11
  163.7 4.4 %collective-permute-start.13 = (bf16[32,128]{1,0:T(8,128)(2,1)S(1)}, bf16[32,128]{1,0:T(8,128)(2,1)S(1)}, u32[]{:S(2)}, u32[]{:S(2)}) collective-permute-start(bf16[32,128]{1,0:T(8,128)(2,1)S(1)} %collective-permute-done.11), channel_id=1, source_target_pairs={{0,15},{1,0},{2,1},{3,2},{4,3},{5,4},{6,5},{7,6},{8,7},{9,8},{10,9... | collective-permute-start | bytes 24584 | tf_op jit(solution)/shard_map/ppermute | solution.py:37
  168.1 1.3 collective-permute-done.12
  169.4 0.0 collective-permute-start.14
  169.5 5.7 %collective-permute-done.14 = bf16[32,128]{1,0:T(8,128)(2,1)S(1)} collective-permute-done((bf16[32,128]{1,0:T(8,128)(2,1)S(1)}, bf16[32,128]{1,0:T(8,128)(2,1)S(1)}, u32[]{:S(2)}, u32[]{:S(2)}) %collective-permute-start.14) | collective-permute-done | bytes 8224 | tf_op jit(solution)/shard_map/ppermute | solution.py:27
  175.2 4.5 %fusion.19 = f32[512,4096]{0,1:T(8,128)} fusion(bf16[512,128]{1,0:T(8,128)(2,1)S(1)} %constant_dynamic-update-slice_fusion, bf16[4096,128]{1,0:T(8,128)(2,1)S(1)} %copy-done), kind=kOutput, calls=%fused_computation.50 | convolution fusion | flops 536870912 | bytes 9568256 | tf_op jit(solution)/shard_map/jp,tp->jt/dot_general | solution.py:61
  179.7 29.9 %scatter_custom_fusion = f32[128,512]{1,0:T(8,128)S(1)} fusion(s32[4096]{0:T(1024)S(1)} %copy-done.3, f32[512,4096]{0,1:T(8,128)} %fusion.19, f32[]{:T(128)} %constant.103.clone.1), kind=kCustom, calls=%fused_computation.1 | custom fusion | flops 2097152 | bytes 8650756 | tf_op jit(solution)/shard_map/scatter-max | solution.py:62
  209.6 0.9 convolution_divide_fusion
  (29 shorter events, 0.2 us)
Async XLA Ops:
  6.5 168.7 %copy-start = (bf16[4096,128]{1,0:T(8,128)(2,1)S(1)}, bf16[4096,128]{1,0:T(8,128)(2,1)}, u32[]{:S(2)}) copy-start(bf16[4096,128]{1,0:T(8,128)(2,1)} %param.16) | copy-start | bytes 3145732
  6.5 43.4 %all-gather.2.cloned.1.call-start = ((), (), s32[]{:S(2)}) async-start(), calls=%async_computation.1 | async-start | bytes 1114112 | tf_op jit(solution)/shard_map/all_gather | solution.py:101
  7.3 119.3 %reduce-scatter.2.cloned.1.call-start = ((), (), s32[]{:S(2)}) async-start(), calls=%async_computation.2 | async-start | bytes 2228224 | tf_op jit(solution)/shard_map/reduce_scatter | solution.py:106
  51.4 16.6 %copy-start.4 = (s32[512]{0:T(512)S(1)}, s32[512]{0:T(512)}, u32[]{:S(2)}) copy-start(s32[512]{0:T(512)} %param.15) | copy-start | bytes 6148
  51.4 16.7 %copy-start.3 = (s32[4096]{0:T(1024)S(1)}, s32[4096]{0:T(1024)}, u32[]{:S(2)}) copy-start(s32[4096]{0:T(1024)} %param.17) | copy-start | bytes 49156
  51.4 75.1 %copy-start.1 = (bf16[32,1024]{1,0:T(8,128)(2,1)S(1)}, bf16[32,1024]{1,0:T(8,128)(2,1)}, u32[]{:S(2)}) copy-start(bf16[32,1024]{1,0:T(8,128)(2,1)} %param.9) | copy-start | bytes 196612
  51.5 76.2 %copy-start.2 = (bf16[1024,128]{1,0:T(8,128)(2,1)S(1)}, bf16[1024,128]{1,0:T(8,128)(2,1)}, u32[]{:S(2)}) copy-start(bf16[1024,128]{1,0:T(8,128)(2,1)} %param.14) | copy-start | bytes 786436
  51.5 76.2 %copy-start.5 = (f32[1024]{0:T(1024)S(1)}, f32[1024]{0:T(1024)}, u32[]{:S(2)}) copy-start(f32[1024]{0:T(1024)} %param.13) | copy-start | bytes 12292
  129.0 5.8 %collective-permute-start = (bf16[32,128]{1,0:T(8,128)(2,1)S(1)}, bf16[32,128]{1,0:T(8,128)(2,1)S(1)}, u32[]{:S(2)}, u32[]{:S(2)}) collective-permute-start(bf16[32,128]{1,0:T(8,128)(2,1)S(1)} %get-tuple-element.6), channel_id=1, source_target_pairs={{0,1},{1,2},{2,3},{3,4},{4,5},{5,6},{6,7},{7,8},{8,9},{9,10},{10,1... | collective-permute-start | bytes 24584 | tf_op jit(solution)/shard_map/ppermute | solution.py:27
  129.8 5.0 %collective-permute-start.1 = (bf16[32,128]{1,0:T(8,128)(2,1)S(1)}, bf16[32,128]{1,0:T(8,128)(2,1)S(1)}, u32[]{:S(2)}, u32[]{:S(2)}) collective-permute-start(bf16[32,128]{1,0:T(8,128)(2,1)S(1)} %get-tuple-element.6), channel_id=1, source_target_pairs={{0,15},{1,0},{2,1},{3,2},{4,3},{5,4},{6,5},{7,6},{8,7},{9,8},{10,9... | collective-permute-start | bytes 24584 | tf_op jit(solution)/shard_map/ppermute | solution.py:37
  134.8 5.8 %collective-permute-start.2 = (bf16[32,128]{1,0:T(8,128)(2,1)S(1)}, bf16[32,128]{1,0:T(8,128)(2,1)S(1)}, u32[]{:S(2)}, u32[]{:S(2)}) collective-permute-start(bf16[32,128]{1,0:T(8,128)(2,1)S(1)} %collective-permute-done), channel_id=1, source_target_pairs={{0,1},{1,2},{2,3},{3,4},{4,5},{5,6},{6,7},{7,8},{8,9},{9,10},{10,1... | collective-permute-start | bytes 24584 | tf_op jit(solution)/shard_map/ppermute | solution.py:27
  134.8 5.8 %collective-permute-start.3 = (bf16[32,128]{1,0:T(8,128)(2,1)S(1)}, bf16[32,128]{1,0:T(8,128)(2,1)S(1)}, u32[]{:S(2)}, u32[]{:S(2)}) collective-permute-start(bf16[32,128]{1,0:T(8,128)(2,1)S(1)} %collective-permute-done.1), channel_id=1, source_target_pairs={{0,15},{1,0},{2,1},{3,2},{4,3},{5,4},{6,5},{7,6},{8,7},{9,8},{10,9... | collective-permute-start | bytes 24584 | tf_op jit(solution)/shard_map/ppermute | solution.py:37
  140.6 5.8 %collective-permute-start.4 = (bf16[32,128]{1,0:T(8,128)(2,1)S(1)}, bf16[32,128]{1,0:T(8,128)(2,1)S(1)}, u32[]{:S(2)}, u32[]{:S(2)}) collective-permute-start(bf16[32,128]{1,0:T(8,128)(2,1)S(1)} %collective-permute-done.2), channel_id=1, source_target_pairs={{0,1},{1,2},{2,3},{3,4},{4,5},{5,6},{6,7},{7,8},{8,9},{9,10},{10,1... | collective-permute-start | bytes 24584 | tf_op jit(solution)/shard_map/ppermute | solution.py:27
  140.6 5.8 %collective-permute-start.5 = (bf16[32,128]{1,0:T(8,128)(2,1)S(1)}, bf16[32,128]{1,0:T(8,128)(2,1)S(1)}, u32[]{:S(2)}, u32[]{:S(2)}) collective-permute-start(bf16[32,128]{1,0:T(8,128)(2,1)S(1)} %collective-permute-done.3), channel_id=1, source_target_pairs={{0,15},{1,0},{2,1},{3,2},{4,3},{5,4},{6,5},{7,6},{8,7},{9,8},{10,9... | collective-permute-start | bytes 24584 | tf_op jit(solution)/shard_map/ppermute | solution.py:37
  146.3 5.8 %collective-permute-start.6 = (bf16[32,128]{1,0:T(8,128)(2,1)S(1)}, bf16[32,128]{1,0:T(8,128)(2,1)S(1)}, u32[]{:S(2)}, u32[]{:S(2)}) collective-permute-start(bf16[32,128]{1,0:T(8,128)(2,1)S(1)} %collective-permute-done.4), channel_id=1, source_target_pairs={{0,1},{1,2},{2,3},{3,4},{4,5},{5,6},{6,7},{7,8},{8,9},{9,10},{10,1... | collective-permute-start | bytes 24584 | tf_op jit(solution)/shard_map/ppermute | solution.py:27
  146.4 5.8 %collective-permute-start.7 = (bf16[32,128]{1,0:T(8,128)(2,1)S(1)}, bf16[32,128]{1,0:T(8,128)(2,1)S(1)}, u32[]{:S(2)}, u32[]{:S(2)}) collective-permute-start(bf16[32,128]{1,0:T(8,128)(2,1)S(1)} %collective-permute-done.5), channel_id=1, source_target_pairs={{0,15},{1,0},{2,1},{3,2},{4,3},{5,4},{6,5},{7,6},{8,7},{9,8},{10,9... | collective-permute-start | bytes 24584 | tf_op jit(solution)/shard_map/ppermute | solution.py:37
  152.1 5.8 %collective-permute-start.8 = (bf16[32,128]{1,0:T(8,128)(2,1)S(1)}, bf16[32,128]{1,0:T(8,128)(2,1)S(1)}, u32[]{:S(2)}, u32[]{:S(2)}) collective-permute-start(bf16[32,128]{1,0:T(8,128)(2,1)S(1)} %collective-permute-done.6), channel_id=1, source_target_pairs={{0,1},{1,2},{2,3},{3,4},{4,5},{5,6},{6,7},{7,8},{8,9},{9,10},{10,1... | collective-permute-start | bytes 24584 | tf_op jit(solution)/shard_map/ppermute | solution.py:27
  152.1 5.8 %collective-permute-start.9 = (bf16[32,128]{1,0:T(8,128)(2,1)S(1)}, bf16[32,128]{1,0:T(8,128)(2,1)S(1)}, u32[]{:S(2)}, u32[]{:S(2)}) collective-permute-start(bf16[32,128]{1,0:T(8,128)(2,1)S(1)} %collective-permute-done.7), channel_id=1, source_target_pairs={{0,15},{1,0},{2,1},{3,2},{4,3},{5,4},{6,5},{7,6},{8,7},{9,8},{10,9... | collective-permute-start | bytes 24584 | tf_op jit(solution)/shard_map/ppermute | solution.py:37
  157.9 5.8 %collective-permute-start.10 = (bf16[32,128]{1,0:T(8,128)(2,1)S(1)}, bf16[32,128]{1,0:T(8,128)(2,1)S(1)}, u32[]{:S(2)}, u32[]{:S(2)}) collective-permute-start(bf16[32,128]{1,0:T(8,128)(2,1)S(1)} %collective-permute-done.8), channel_id=1, source_target_pairs={{0,1},{1,2},{2,3},{3,4},{4,5},{5,6},{6,7},{7,8},{8,9},{9,10},{10,1... | collective-permute-start | bytes 24584 | tf_op jit(solution)/shard_map/ppermute | solution.py:27
  157.9 5.8 %collective-permute-start.11 = (bf16[32,128]{1,0:T(8,128)(2,1)S(1)}, bf16[32,128]{1,0:T(8,128)(2,1)S(1)}, u32[]{:S(2)}, u32[]{:S(2)}) collective-permute-start(bf16[32,128]{1,0:T(8,128)(2,1)S(1)} %collective-permute-done.9), channel_id=1, source_target_pairs={{0,15},{1,0},{2,1},{3,2},{4,3},{5,4},{6,5},{7,6},{8,7},{9,8},{10,9... | collective-permute-start | bytes 24584 | tf_op jit(solution)/shard_map/ppermute | solution.py:37
  163.7 5.8 %collective-permute-start.12 = (bf16[32,128]{1,0:T(8,128)(2,1)S(1)}, bf16[32,128]{1,0:T(8,128)(2,1)S(1)}, u32[]{:S(2)}, u32[]{:S(2)}) collective-permute-start(bf16[32,128]{1,0:T(8,128)(2,1)S(1)} %collective-permute-done.10), channel_id=1, source_target_pairs={{0,1},{1,2},{2,3},{3,4},{4,5},{5,6},{6,7},{7,8},{8,9},{9,10},{10,1... | collective-permute-start | bytes 24584 | tf_op jit(solution)/shard_map/ppermute | solution.py:27
  163.7 5.8 %collective-permute-start.13 = (bf16[32,128]{1,0:T(8,128)(2,1)S(1)}, bf16[32,128]{1,0:T(8,128)(2,1)S(1)}, u32[]{:S(2)}, u32[]{:S(2)}) collective-permute-start(bf16[32,128]{1,0:T(8,128)(2,1)S(1)} %collective-permute-done.11), channel_id=1, source_target_pairs={{0,15},{1,0},{2,1},{3,2},{4,3},{5,4},{6,5},{7,6},{8,7},{9,8},{10,9... | collective-permute-start | bytes 24584 | tf_op jit(solution)/shard_map/ppermute | solution.py:37
  169.4 5.8 %collective-permute-start.14 = (bf16[32,128]{1,0:T(8,128)(2,1)S(1)}, bf16[32,128]{1,0:T(8,128)(2,1)S(1)}, u32[]{:S(2)}, u32[]{:S(2)}) collective-permute-start(bf16[32,128]{1,0:T(8,128)(2,1)S(1)} %collective-permute-done.12), channel_id=1, source_target_pairs={{0,1},{1,2},{2,3},{3,4},{4,5},{5,6},{6,7},{7,8},{8,9},{9,10},{10,1... | collective-permute-start | bytes 24584 | tf_op jit(solution)/shard_map/ppermute | solution.py:27
Sparse Core Ops, SparseCore 0:
  9.5 40.3 all-gather.1
  68.0 58.5 reduce-scatter.1
